TPU v7x, 32 devices: a whole 2x2x4 slice. The times are simulated.
32 devices in a mesh: row: 4 (over z), col: 8 (over y, x, core).
Axes of the slice: x: 2, y: 2, z: 4, core: 2. Of those that a mesh axis runs over, the one named last changes fastest.
Arguments:
- features: bfloat16 [8, 1024, 256], P('col', 'row'), may hold values from -6 to 6
- weight: bfloat16 [256, 256], replicated, may hold values from -0.375 to 0.375
- cotangent: bfloat16 [8192, 256], P(('row', 'col')), may hold values from -6 to 6
- blk_vals: bfloat16 [4, 8, 192, 128, 128], P('row', 'col'), may hold values from -0.0546875 to 0.0546875
- blk_rows: int32 [4, 8, 192], P('row', 'col'), may hold values from 0 to 15
- blk_cols: int32 [4, 8, 192], P('row', 'col'), may hold values from 0 to 7
- blk_count: int32 [4, 8], P('row', 'col'), may hold values from 24 to 192, as said below
Outputs:
- activated: bfloat16 [8192, 256], P(('row', 'col'))
- grad_weight: float32 [256, 256], replicated
- grad_features: bfloat16 [8, 1024, 256], P('col', 'row')
Inputs may be any that keep to these rules, and one draw needn't show every extreme that they name: Only the first blk_count slots of a panel pair are used; a pair whose row and column node ranges intersect uses all 192, every other pair at most 96.
All inputs are finite; a program needn't handle non-finite values.
Results may differ from a plain program's by a relative error of at most 0.0059.
Values may be sent and summed in bfloat16 or wider, within the bound.
A program may use at most 128 MiB of HBM per device.

v0:
```python
import jax
import jax.numpy as jnp
from jax import lax
from jax.sharding import PartitionSpec as P


def block_terms(values, index, source, live_count, transpose):
    total_slots = values.shape[0]
    group = 64
    width = source.shape[-1]
    side = values.shape[-1]
    if transpose:
        form = "bji,bjf->bif"
    else:
        form = "bij,bjf->bif"

    def one_group(group_index, buffer):
        first = group_index * group
        block_vals = lax.dynamic_slice_in_dim(values, first, group, 0)
        block_ids = lax.dynamic_slice_in_dim(index, first, group, 0)
        picked = jnp.take(source, block_ids, axis=0)
        product = jnp.einsum(form, block_vals, picked, preferred_element_type=jnp.float32)
        alive = first + jnp.arange(group, dtype=jnp.int32) < live_count
        product = jnp.where(alive[:, None, None], product, 0.0)
        return lax.dynamic_update_slice_in_dim(buffer, product, first, 0)

    buffer = jnp.zeros((total_slots, side, width), jnp.float32)
    groups = total_slots // group
    return lax.fori_loop(0, groups, one_group, buffer)


def per_device(features, weight, cotangent, blk_vals, blk_rows, blk_cols, blk_count):
    rows_here = cotangent.shape[0]
    width = cotangent.shape[1]
    side = blk_vals.shape[-1]
    row_blocks = rows_here * lax.axis_size("col") // side
    col_blocks = rows_here * lax.axis_size("row") // side
    values = blk_vals[0, 0]
    row_ids = blk_rows[0, 0]
    col_ids = blk_cols[0, 0]
    live_count = blk_count[0, 0]
    panel = lax.all_gather(features, "row", axis=1, tiled=True)
    source = panel.reshape(col_blocks, side, width)
    products = block_terms(values, col_ids, source, live_count, False)
    partial_rows = jax.ops.segment_sum(products, row_ids, num_segments=row_blocks)
    own_rows = lax.psum_scatter(
        partial_rows.reshape(row_blocks * side, width), "col", scatter_dimension=0, tiled=True
    )
    aggregated = own_rows.astype(jnp.bfloat16)
    pre = jnp.dot(aggregated, weight, preferred_element_type=jnp.float32)
    sigma = jax.nn.sigmoid(pre)
    activated = (pre * sigma).astype(jnp.bfloat16)
    grad_pre = (cotangent.astype(jnp.float32) * sigma * (1.0 + pre * (1.0 - sigma))).astype(
        jnp.bfloat16
    )
    local_weight = lax.dot_general(
        aggregated, grad_pre, (((0,), (0,)), ((), ())), preferred_element_type=jnp.float32
    )
    grad_weight = lax.psum(local_weight, ("row", "col"))
    grad_agg = lax.dot_general(
        grad_pre, weight, (((1,), (1,)), ((), ())), preferred_element_type=jnp.float32
    ).astype(jnp.bfloat16)
    grad_rows = lax.all_gather(grad_agg, "col", axis=0, tiled=True)
    grad_source = grad_rows.reshape(row_blocks, side, width)
    back_products = block_terms(values, row_ids, grad_source, live_count, True)
    partial_cols = jax.ops.segment_sum(back_products, col_ids, num_segments=col_blocks)
    own_cols = lax.psum_scatter(
        partial_cols.reshape(col_blocks * side, width), "row", scatter_dimension=0, tiled=True
    )
    grad_features = own_cols.astype(jnp.bfloat16).reshape(1, rows_here, width)
    return (activated, grad_weight, grad_features)


def solution(mesh):
    return jax.shard_map(
        per_device,
        mesh=mesh,
        in_specs=(
            P("col", "row", None),
            P(),
            P(("row", "col"), None),
            P("row", "col", None, None, None),
            P("row", "col", None),
            P("row", "col", None),
            P("row", "col"),
        ),
        out_specs=(P(("row", "col"), None), P(), P("col", "row", None)),
        check_vma=False,
    )
```

profile of v0, /device:TPU:0, one launch (start us, length us, event | category | flops | bytes accessed | tf_op | source)
XLA Modules:
  0.0 423.9 jit_solution(15833494370647342353)
XLA Ops:
  7.2 17.6 %all_gather.6 = bf16[1,1024,256]{2,1,0:T(8,128)(2,1)S(1)} all-gather(bf16[1,256,256]{2,1,0:T(8,128)(2,1)} %param.11), channel_id=1, replica_groups=mesh['row'=4,'col'=8] {'row'}, dimensions={1}, use_global_device_ids=true | all-gather | bytes 655360 | tf_op jit(solution)/shard_map/all_gather | solution.py:42
  24.8 11.5 %broadcast.44.clone = f32[192,128,256]{2,1,0:T(8,128)} broadcast(f32[]{:T(128)} %constant.131.clone.1), dimensions={} | broadcast | bytes 25165828 | tf_op jit(solution)/shard_map/broadcast.3
  36.3 32.7 %while.26 = (s32[]{:T(128)}, f32[192,128,256]{2,1,0:T(8,128)}, s32[]{:T(128)}, bf16[192,128,128]{2,1,0:T(8,128)(2,1)}, s32[192]{0:T(256)S(1)}, /*index=5*/bf16[8...) while((s32[]{:T(128)}, f32[192,128,256]{2,1,0:T(8,128)}, s32[]{:T(128)}, ...), condition=%wide.region_1.0_spmd, body=%wide.region_0.1_spmd.sunk | while | flops 541066752 | bytes 23075232 | solution.py:29
  37.1 2.8 gather_fusion
  39.8 7.4 %select_dynamic-update-slice_fusion.4 = f32[192,128,256]{2,1,0:T(8,128)} fusion(f32[192,128,256]{2,1,0:T(8,128)} %get-tuple-element.358, s32[]{:T(128)S(6)} %select_n.88, pred[64]{0:T(512)(128)(4,1)S(1)} %get-tuple-element.335, bf16[64,128,256]{2,1,0:T(8,128)(2,1)} %gather_fusion, pred[64]{0:T(512)(128)(4,1)S(1)} %get-tuple-element.337, ...), kind=kOutput, calls=%fused_computation.4.clone.1 | convolution fusion | flops 541065216 | bytes 14681216 | tf_op jit(solution)/shard_map/while/body/eval_jaxpr/bij,bjf->bif/dot_general | solution.py:22
  47.9 2.8 gather_fusion
  50.7 7.4 %select_dynamic-update-slice_fusion.4 = f32[192,128,256]{2,1,0:T(8,128)} fusion(f32[192,128,256]{2,1,0:T(8,128)} %get-tuple-element.358, s32[]{:T(128)S(6)} %select_n.88, pred[64]{0:T(512)(128)(4,1)S(1)} %get-tuple-element.335, bf16[64,128,256]{2,1,0:T(8,128)(2,1)} %gather_fusion, pred[64]{0:T(512)(128)(4,1)S(1)} %get-tuple-element.337, ...), kind=kOutput, calls=%fused_computation.4.clone.1 | convolution fusion | flops 541065216 | bytes 14681216 | tf_op jit(solution)/shard_map/while/body/eval_jaxpr/bij,bjf->bif/dot_general | solution.py:22
  58.8 2.8 gather_fusion
  61.6 7.4 %select_dynamic-update-slice_fusion.4 = f32[192,128,256]{2,1,0:T(8,128)} fusion(f32[192,128,256]{2,1,0:T(8,128)} %get-tuple-element.358, s32[]{:T(128)S(6)} %select_n.88, pred[64]{0:T(512)(128)(4,1)S(1)} %get-tuple-element.335, bf16[64,128,256]{2,1,0:T(8,128)(2,1)} %gather_fusion, pred[64]{0:T(512)(128)(4,1)S(1)} %get-tuple-element.337, ...), kind=kOutput, calls=%fused_computation.4.clone.1 | convolution fusion | flops 541065216 | bytes 14681216 | tf_op jit(solution)/shard_map/while/body/eval_jaxpr/bij,bjf->bif/dot_general | solution.py:22
  69.2 36.1 %scatter_fusion = f32[16,128,256]{2,1,0:T(8,128)S(1)} fusion(f32[16,128,256]{2,1,0:T(8,128)S(1)} %broadcast_in_dim.108, s32[192]{0:T(256)S(1)} %bitcast.22, f32[192,128,256]{2,1,0:T(8,128)} %get-tuple-element.221), kind=kCustom, calls=%fused_computation.2 | custom fusion | flops 6291456 | bytes 75498240 | tf_op jit(solution)/shard_map/scatter-add | solution.py:45
  106.7 43.0 %reduce-scatter.3.cloned.1.call-done = f32[256,256]{1,0:T(8,128)} async-done(((f32[2048,256]{1,0:T(8,128)}), f32[256,256]{1,0:T(8,128)}) %reduce-scatter.3.cloned.1.call-update) | async-done | bytes 262160 | tf_op jit(solution)/shard_map/reduce_scatter | solution.py:46
  152.5 8.6 %copy.10 = bf16[1,1,192,128,128]{3,4,2,1,0:T(8,128)(2,1)} copy(bf16[1,1,192,128,128]{4,3,2,1,0:T(8,128)(2,1)} %bitcast.20) | data formatting | bytes 12582912 | tf_op args[3]
  161.0 14.9 %all-gather.2.cloned.1.call-done = bf16[2048,256]{1,0:T(8,128)(2,1)} async-done(((bf16[256,256]{1,0:T(8,128)(2,1)}), bf16[2048,256]{1,0:T(8,128)(2,1)}) %all-gather.2.cloned.1.call-update) | async-done | bytes 1048592 | tf_op jit(solution)/shard_map/all_gather | solution.py:63
  176.0 11.5 %broadcast.44 = f32[192,128,256]{2,1,0:T(8,128)} broadcast(f32[]{:T(128)} %constant.131.clone.1), dimensions={} | broadcast | bytes 25165828 | tf_op jit(solution)/shard_map/broadcast.3
  187.4 32.7 %while.27 = (s32[]{:T(128)}, f32[192,128,256]{2,1,0:T(8,128)}, s32[]{:T(128)}, bf16[192,128,128]{1,2,0:T(8,128)(2,1)}, s32[192]{0:T(256)S(1)}, /*index=5*/bf16[1...) while((s32[]{:T(128)}, f32[192,128,256]{2,1,0:T(8,128)}, s32[]{:T(128)}, ...), condition=%wide.region_6.7_spmd, body=%wide.region_5.6_spmd.sunk | while | flops 541066752 | bytes 23075232 | solution.py:29
  188.2 2.8 gather_fusion.1
  191.0 7.4 %select_dynamic-update-slice_fusion.5 = f32[192,128,256]{2,1,0:T(8,128)} fusion(f32[192,128,256]{2,1,0:T(8,128)} %get-tuple-element.388, s32[]{:T(128)S(6)} %select_n.91, pred[64]{0:T(512)(128)(4,1)S(1)} %get-tuple-element.344, bf16[64,128,256]{2,1,0:T(8,128)(2,1)} %gather_fusion.1, pred[64]{0:T(512)(128)(4,1)S(1)} %get-tuple-element.346, ...), kind=kOutput, calls=%fused_computation.16.clone.1 | convolution fusion | flops 541065216 | bytes 14681216 | tf_op jit(solution)/shard_map/while/body/eval_jaxpr/bji,bjf->bif/dot_general | solution.py:22
  199.1 2.8 gather_fusion.1
  201.8 7.4 %select_dynamic-update-slice_fusion.5 = f32[192,128,256]{2,1,0:T(8,128)} fusion(f32[192,128,256]{2,1,0:T(8,128)} %get-tuple-element.388, s32[]{:T(128)S(6)} %select_n.91, pred[64]{0:T(512)(128)(4,1)S(1)} %get-tuple-element.344, bf16[64,128,256]{2,1,0:T(8,128)(2,1)} %gather_fusion.1, pred[64]{0:T(512)(128)(4,1)S(1)} %get-tuple-element.346, ...), kind=kOutput, calls=%fused_computation.16.clone.1 | convolution fusion | flops 541065216 | bytes 14681216 | tf_op jit(solution)/shard_map/while/body/eval_jaxpr/bji,bjf->bif/dot_general | solution.py:22
  210.0 2.8 gather_fusion.1
  212.7 7.4 %select_dynamic-update-slice_fusion.5 = f32[192,128,256]{2,1,0:T(8,128)} fusion(f32[192,128,256]{2,1,0:T(8,128)} %get-tuple-element.388, s32[]{:T(128)S(6)} %select_n.91, pred[64]{0:T(512)(128)(4,1)S(1)} %get-tuple-element.344, bf16[64,128,256]{2,1,0:T(8,128)(2,1)} %gather_fusion.1, pred[64]{0:T(512)(128)(4,1)S(1)} %get-tuple-element.346, ...), kind=kOutput, calls=%fused_computation.16.clone.1 | convolution fusion | flops 541065216 | bytes 14681216 | tf_op jit(solution)/shard_map/while/body/eval_jaxpr/bji,bjf->bif/dot_general | solution.py:22
  220.2 36.0 %scatter_fusion.1 = f32[8,128,256]{2,1,0:T(8,128)S(1)} fusion(f32[8,128,256]{2,1,0:T(8,128)S(1)} %broadcast_in_dim.109, s32[192]{0:T(256)S(1)} %get-tuple-element.427, f32[192,128,256]{2,1,0:T(8,128)} %get-tuple-element.222), kind=kCustom, calls=%fused_computation.3 | custom fusion | flops 6291456 | bytes 75498240 | tf_op jit(solution)/shard_map/scatter-add | solution.py:66
  258.2 26.4 %reduce-scatter.5.cloned.1.call-done = f32[256,256]{1,0:T(8,128)} async-done(((f32[1024,256]{1,0:T(8,128)}), f32[256,256]{1,0:T(8,128)}) %reduce-scatter.5.cloned.1.call-update) | async-done | bytes 262160 | tf_op jit(solution)/shard_map/reduce_scatter | solution.py:67
  286.3 129.4 %all-reduce.2.cloned.1.call-done = f32[256,256]{1,0:T(8,128)} async-done(((f32[256,256]{1,0:T(8,128)}), f32[256,256]{1,0:T(8,128)}) %all-reduce.2.cloned.1.call-update) | async-done | bytes 262160 | tf_op jit(solution)/shard_map/psum | solution.py:59
  (45 shorter events, 14.2 us)
Async XLA Ops:
  7.2 142.5 %copy-start = (bf16[256,256]{1,0:T(8,128)(2,1)S(1)}, bf16[256,256]{1,0:T(8,128)(2,1)}, u32[]{:S(2)}) copy-start(bf16[256,256]{1,0:T(8,128)(2,1)} %param.12) | copy-start | bytes 393220
  7.2 142.5 %reduce-scatter.3.cloned.1.call-start = ((), (), s32[]{:S(2)}) async-start(), calls=%async_computation.2 | async-start | bytes 2359296 | tf_op jit(solution)/shard_map/reduce_scatter | solution.py:46
  24.8 11.5 %copy-start.7 = (s32[1,1,192]{2,1,0:T(1,128)S(1)}, s32[1,1,192]{2,1,0:T(1,128)}, u32[]{:S(2)}) copy-start(s32[1,1,192]{2,1,0:T(1,128)} %param.16) | copy-start | bytes 2308
  36.3 32.9 %copy-start.6 = (s32[1,1,192]{2,1,0:T(1,128)S(1)}, s32[1,1,192]{2,1,0:T(1,128)}, u32[]{:S(2)}) copy-start(s32[1,1,192]{2,1,0:T(1,128)} %param.15) | copy-start | bytes 2308
  69.2 80.4 %copy-start.8 = (bf16[256,256]{1,0:T(8,128)(2,1)S(1)}, bf16[256,256]{1,0:T(8,128)(2,1)}, u32[]{:S(2)}) copy-start(bf16[256,256]{1,0:T(8,128)(2,1)} %param.13) | copy-start | bytes 393220
  105.3 1.3 copy-start.4
  106.6 69.3 %all-gather.2.cloned.1.call-start = ((), (), s32[]{:S(2)}) async-start(), calls=%async_computation.4 | async-start | bytes 1179648 | tf_op jit(solution)/shard_map/all_gather | solution.py:63
  152.4 132.2 %reduce-scatter.5.cloned.1.call-start = ((), (), s32[]{:S(2)}) async-start(), calls=%async_computation.5 | async-start | bytes 1310720 | tf_op jit(solution)/shard_map/reduce_scatter | solution.py:67
  176.0 11.5 %copy-start.3 = (bf16[2048,256]{1,0:T(8,128)(2,1)S(1)}, bf16[2048,256]{1,0:T(8,128)(2,1)}, u32[]{:S(2)}) copy-start(bf16[2048,256]{1,0:T(8,128)(2,1)} %all-gather.2.cloned.1.call-done) | copy-start | bytes 3145732
  220.2 37.1 %copy-start.5 = (f32[256,256]{1,0:T(8,128)S(1)}, f32[256,256]{1,0:T(8,128)}, u32[]{:S(2)}) copy-start(f32[256,256]{1,0:T(8,128)} %reduce-scatter.3.cloned.1.call-done) | copy-start | bytes 786436
  220.2 197.1 %copy-start.1 = (bf16[256,256]{1,0:T(8,128)(2,1)S(1)}, bf16[256,256]{1,0:T(8,128)(2,1)}, u32[]{:S(2)}) copy-start(bf16[256,256]{1,0:T(8,128)(2,1)} %param.12) | copy-start | bytes 393220
  256.2 1.0 copy-start.2
  257.2 158.5 %all-reduce.2.cloned.1.call-start = ((), (), s32[]{:S(2)}) async-start(), calls=%async_computation.3 | async-start | bytes 524288 | tf_op jit(solution)/shard_map/psum | solution.py:59
Sparse Core Ops, SparseCore 0:
  106.7 42.8 reduce-scatter.2
  152.6 23.3 all-gather.1
  257.3 27.2 reduce-scatter.4
  290.6 125.0 all-reduce.1
where the time goes:
time: 425 us; the launch traced here: 424 us
  waiting for transfers between devices  214 us (50%)
  other arithmetic  78.1 us (18%)
  local copies, waits for them, and re-layouts  52.5 us (12%)
  matrix products  47.9 us (11%)
  blocking collectives  17.6 us (4%)
  between operations  13.9 us (3%)
    psum x1, waiting for transfers between devices, per_device(): grad_weight = lax.psum(local_weight, ('row', 'col'))  129 us
    dot_general x6, matrix products, one_group(): jnp.einsum(form, block_vals, picked, preferred_element_type=jnp.float32)  44.3 us
    reduce_scatter x1, waiting for transfers between devices, per_device(): lax.psum_scatter(partial_rows.reshape(row_blocks * side, width), 'col', s...  43 us
    scatter-add x1, other arithmetic, per_device(): jax.ops.segment_sum(products, row_ids, num_segments=row_blocks)  36.1 us
    scatter-add x1, other arithmetic, per_device(): jax.ops.segment_sum(back_products, col_ids, num_segments=col_blocks)  36 us
    reduce_scatter x1, waiting for transfers between devices, per_device(): lax.psum_scatter(partial_cols.reshape(col_blocks * side, width), 'row', s...  26.4 us
    another operation x2, local copies, waits for them, and re-layouts  23 us
    all_gather x1, blocking collectives, per_device(): panel = lax.all_gather(features, 'row', axis=1, tiled=True)  17.6 us
  transfers between devices with their start and end apart: 4, of which 4 were waited for; matrix products, arithmetic and copies ran while one was open for 3% of the time, Pallas kernels for 0%

commit v1 on v0

--- a/solution.py
+++ b/solution.py
@@ -56,7 +56,7 @@
     local_weight = lax.dot_general(
         aggregated, grad_pre, (((0,), (0,)), ((), ())), preferred_element_type=jnp.float32
     )
-    grad_weight = lax.psum(local_weight, ("row", "col"))
+    grad_weight = lax.psum(lax.psum(local_weight, "col"), "row")
     grad_agg = lax.dot_general(
         grad_pre, weight, (((1,), (1,)), ((), ())), preferred_element_type=jnp.float32
     ).astype(jnp.bfloat16)

time: 425 us -> 331 us (0.78)
  waiting for transfers between devices: 214 us -> 119 us
    psum x1 -> x2, waiting for transfers between devices: 129 us -> 34.7 us  [per_device(): grad_weight = lax.psum(lax.psum(local_weight, 'col'), 'row')]
  transfers between devices with their start and end apart: 4 -> 5, of which waited for: 4 -> 4; matrix products, arithmetic and copies ran while one was open for 3% -> 28% of each run, Pallas kernels for 0% -> 0%
where the time goes in v1:
time: 331 us; the launch traced here: 329 us
  waiting for transfers between devices  119 us (36%)
  other arithmetic  78.1 us (24%)
  local copies, waits for them, and re-layouts  52.6 us (16%)
  matrix products  48 us (15%)
  blocking collectives  17.6 us (5%)
  between operations  13.9 us (4%)
    dot_general x6, matrix products, one_group(): jnp.einsum(form, block_vals, picked, preferred_element_type=jnp.float32)  44.3 us
    reduce_scatter x1, waiting for transfers between devices, per_device(): lax.psum_scatter(partial_rows.reshape(row_blocks * side, width), 'col', s...  43 us
    scatter-add x1, other arithmetic, per_device(): jax.ops.segment_sum(products, row_ids, num_segments=row_blocks)  36.1 us
    scatter-add x1, other arithmetic, per_device(): jax.ops.segment_sum(back_products, col_ids, num_segments=col_blocks)  36 us
    psum x2, waiting for transfers between devices, per_device(): grad_weight = lax.psum(lax.psum(local_weight, 'col'), 'row')  34.7 us
    reduce_scatter x1, waiting for transfers between devices, per_device(): lax.psum_scatter(partial_cols.reshape(col_blocks * side, width), 'row', s...  26.9 us
    another operation x2, local copies, waits for them, and re-layouts  23 us
    all_gather x1, blocking collectives, per_device(): panel = lax.all_gather(features, 'row', axis=1, tiled=True)  17.6 us
  transfers between devices with their start and end apart: 5, of which 4 were waited for; matrix products, arithmetic and copies ran while one was open for 28% of the time, Pallas kernels for 0%

profile of v1, /device:TPU:0, one launch (start us, length us, event | category | flops | bytes accessed | tf_op | source)
XLA Modules:
  0.0 329.3 jit_solution(2362421956407925268)
XLA Ops:
  7.2 17.6 %all_gather.6 = bf16[1,1024,256]{2,1,0:T(8,128)(2,1)S(1)} all-gather(bf16[1,256,256]{2,1,0:T(8,128)(2,1)} %param.11), channel_id=1, replica_groups=mesh['row'=4,'col'=8] {'row'}, dimensions={1}, use_global_device_ids=true | all-gather | bytes 655360 | tf_op jit(solution)/shard_map/all_gather | solution.py:42
  24.8 11.5 %broadcast.44.clone = f32[192,128,256]{2,1,0:T(8,128)} broadcast(f32[]{:T(128)} %constant.131.clone.1), dimensions={} | broadcast | bytes 25165828 | tf_op jit(solution)/shard_map/broadcast.3
  36.3 32.7 %while.26 = (s32[]{:T(128)}, f32[192,128,256]{2,1,0:T(8,128)}, s32[]{:T(128)}, bf16[192,128,128]{2,1,0:T(8,128)(2,1)}, s32[192]{0:T(256)S(1)}, /*index=5*/bf16[8...) while((s32[]{:T(128)}, f32[192,128,256]{2,1,0:T(8,128)}, s32[]{:T(128)}, ...), condition=%wide.region_1.0_spmd, body=%wide.region_0.1_spmd.sunk | while | flops 541066752 | bytes 23075232 | solution.py:29
  37.1 2.8 gather_fusion
  39.8 7.4 %select_dynamic-update-slice_fusion.4 = f32[192,128,256]{2,1,0:T(8,128)} fusion(f32[192,128,256]{2,1,0:T(8,128)} %get-tuple-element.358, s32[]{:T(128)S(6)} %select_n.88, pred[64]{0:T(512)(128)(4,1)S(1)} %get-tuple-element.335, bf16[64,128,256]{2,1,0:T(8,128)(2,1)} %gather_fusion, pred[64]{0:T(512)(128)(4,1)S(1)} %get-tuple-element.337, ...), kind=kOutput, calls=%fused_computation.4.clone.1 | convolution fusion | flops 541065216 | bytes 14681216 | tf_op jit(solution)/shard_map/while/body/eval_jaxpr/bij,bjf->bif/dot_general | solution.py:22
  47.9 2.8 gather_fusion
  50.7 7.4 %select_dynamic-update-slice_fusion.4 = f32[192,128,256]{2,1,0:T(8,128)} fusion(f32[192,128,256]{2,1,0:T(8,128)} %get-tuple-element.358, s32[]{:T(128)S(6)} %select_n.88, pred[64]{0:T(512)(128)(4,1)S(1)} %get-tuple-element.335, bf16[64,128,256]{2,1,0:T(8,128)(2,1)} %gather_fusion, pred[64]{0:T(512)(128)(4,1)S(1)} %get-tuple-element.337, ...), kind=kOutput, calls=%fused_computation.4.clone.1 | convolution fusion | flops 541065216 | bytes 14681216 | tf_op jit(solution)/shard_map/while/body/eval_jaxpr/bij,bjf->bif/dot_general | solution.py:22
  58.8 2.8 gather_fusion
  61.6 7.4 %select_dynamic-update-slice_fusion.4 = f32[192,128,256]{2,1,0:T(8,128)} fusion(f32[192,128,256]{2,1,0:T(8,128)} %get-tuple-element.358, s32[]{:T(128)S(6)} %select_n.88, pred[64]{0:T(512)(128)(4,1)S(1)} %get-tuple-element.335, bf16[64,128,256]{2,1,0:T(8,128)(2,1)} %gather_fusion, pred[64]{0:T(512)(128)(4,1)S(1)} %get-tuple-element.337, ...), kind=kOutput, calls=%fused_computation.4.clone.1 | convolution fusion | flops 541065216 | bytes 14681216 | tf_op jit(solution)/shard_map/while/body/eval_jaxpr/bij,bjf->bif/dot_general | solution.py:22
  69.2 36.1 %scatter_fusion = f32[16,128,256]{2,1,0:T(8,128)S(1)} fusion(f32[16,128,256]{2,1,0:T(8,128)S(1)} %broadcast_in_dim.108, s32[192]{0:T(256)S(1)} %bitcast.22, f32[192,128,256]{2,1,0:T(8,128)} %get-tuple-element.221), kind=kCustom, calls=%fused_computation.2 | custom fusion | flops 6291456 | bytes 75498240 | tf_op jit(solution)/shard_map/scatter-add | solution.py:45
  106.7 43.0 %reduce-scatter.3.cloned.1.call-done = f32[256,256]{1,0:T(8,128)} async-done(((f32[2048,256]{1,0:T(8,128)}), f32[256,256]{1,0:T(8,128)}) %reduce-scatter.3.cloned.1.call-update) | async-done | bytes 262160 | tf_op jit(solution)/shard_map/reduce_scatter | solution.py:46
  152.5 8.6 %copy.10 = bf16[1,1,192,128,128]{3,4,2,1,0:T(8,128)(2,1)} copy(bf16[1,1,192,128,128]{4,3,2,1,0:T(8,128)(2,1)} %bitcast.20) | data formatting | bytes 12582912 | tf_op args[3]
  162.1 13.9 %all-gather.2.cloned.1.call-done = bf16[2048,256]{1,0:T(8,128)(2,1)} async-done(((bf16[256,256]{1,0:T(8,128)(2,1)}), bf16[2048,256]{1,0:T(8,128)(2,1)}) %all-gather.2.cloned.1.call-update) | async-done | bytes 1048592 | tf_op jit(solution)/shard_map/all_gather | solution.py:63
  176.0 11.6 %broadcast.44 = f32[192,128,256]{2,1,0:T(8,128)} broadcast(f32[]{:T(128)} %constant.131.clone.1), dimensions={} | broadcast | bytes 25165828 | tf_op jit(solution)/shard_map/broadcast.3
  187.5 32.7 %while.27 = (s32[]{:T(128)}, f32[192,128,256]{2,1,0:T(8,128)}, s32[]{:T(128)}, bf16[192,128,128]{1,2,0:T(8,128)(2,1)}, s32[192]{0:T(256)S(1)}, /*index=5*/bf16[1...) while((s32[]{:T(128)}, f32[192,128,256]{2,1,0:T(8,128)}, s32[]{:T(128)}, ...), condition=%wide.region_7.8_spmd, body=%wide.region_6.7_spmd.sunk | while | flops 541066752 | bytes 23075232 | solution.py:29
  188.2 2.8 gather_fusion.1
  191.0 7.4 %select_dynamic-update-slice_fusion.5 = f32[192,128,256]{2,1,0:T(8,128)} fusion(f32[192,128,256]{2,1,0:T(8,128)} %get-tuple-element.388, s32[]{:T(128)S(6)} %select_n.91, pred[64]{0:T(512)(128)(4,1)S(1)} %get-tuple-element.344, bf16[64,128,256]{2,1,0:T(8,128)(2,1)} %gather_fusion.1, pred[64]{0:T(512)(128)(4,1)S(1)} %get-tuple-element.346, ...), kind=kOutput, calls=%fused_computation.16.clone.1 | convolution fusion | flops 541065216 | bytes 14681216 | tf_op jit(solution)/shard_map/while/body/eval_jaxpr/bji,bjf->bif/dot_general | solution.py:22
  199.1 2.8 gather_fusion.1
  201.9 7.4 %select_dynamic-update-slice_fusion.5 = f32[192,128,256]{2,1,0:T(8,128)} fusion(f32[192,128,256]{2,1,0:T(8,128)} %get-tuple-element.388, s32[]{:T(128)S(6)} %select_n.91, pred[64]{0:T(512)(128)(4,1)S(1)} %get-tuple-element.344, bf16[64,128,256]{2,1,0:T(8,128)(2,1)} %gather_fusion.1, pred[64]{0:T(512)(128)(4,1)S(1)} %get-tuple-element.346, ...), kind=kOutput, calls=%fused_computation.16.clone.1 | convolution fusion | flops 541065216 | bytes 14681216 | tf_op jit(solution)/shard_map/while/body/eval_jaxpr/bji,bjf->bif/dot_general | solution.py:22
  210.1 2.8 gather_fusion.1
  212.8 7.4 %select_dynamic-update-slice_fusion.5 = f32[192,128,256]{2,1,0:T(8,128)} fusion(f32[192,128,256]{2,1,0:T(8,128)} %get-tuple-element.388, s32[]{:T(128)S(6)} %select_n.91, pred[64]{0:T(512)(128)(4,1)S(1)} %get-tuple-element.344, bf16[64,128,256]{2,1,0:T(8,128)(2,1)} %gather_fusion.1, pred[64]{0:T(512)(128)(4,1)S(1)} %get-tuple-element.346, ...), kind=kOutput, calls=%fused_computation.16.clone.1 | convolution fusion | flops 541065216 | bytes 14681216 | tf_op jit(solution)/shard_map/while/body/eval_jaxpr/bji,bjf->bif/dot_general | solution.py:22
  220.3 36.0 %scatter_fusion.1 = f32[8,128,256]{2,1,0:T(8,128)S(1)} fusion(f32[8,128,256]{2,1,0:T(8,128)S(1)} %broadcast_in_dim.109, s32[192]{0:T(256)S(1)} %get-tuple-element.431, f32[192,128,256]{2,1,0:T(8,128)} %get-tuple-element.222), kind=kCustom, calls=%fused_computation.3 | custom fusion | flops 6291456 | bytes 75498240 | tf_op jit(solution)/shard_map/scatter-add | solution.py:66
  257.9 26.9 %reduce-scatter.5.cloned.1.call-done = f32[256,256]{1,0:T(8,128)} async-done(((f32[1024,256]{1,0:T(8,128)}), f32[256,256]{1,0:T(8,128)}) %reduce-scatter.5.cloned.1.call-update) | async-done | bytes 262160 | tf_op jit(solution)/shard_map/reduce_scatter | solution.py:67
  286.4 34.7 %all-reduce.5.cloned.1.call-done = f32[256,256]{1,0:T(8,128)} async-done(((f32[256,256]{1,0:T(8,128)}), f32[256,256]{1,0:T(8,128)}) %all-reduce.5.cloned.1.call-update) | async-done | bytes 262160 | tf_op jit(solution)/shard_map/psum | solution.py:59
  (48 shorter events, 14.8 us)
Async XLA Ops:
  7.2 142.5 %copy-start = (bf16[256,256]{1,0:T(8,128)(2,1)S(1)}, bf16[256,256]{1,0:T(8,128)(2,1)}, u32[]{:S(2)}) copy-start(bf16[256,256]{1,0:T(8,128)(2,1)} %param.12) | copy-start | bytes 393220
  7.2 142.5 %reduce-scatter.3.cloned.1.call-start = ((), (), s32[]{:S(2)}) async-start(), calls=%async_computation.2 | async-start | bytes 2359296 | tf_op jit(solution)/shard_map/reduce_scatter | solution.py:46
  24.8 11.5 %copy-start.7 = (s32[1,1,192]{2,1,0:T(1,128)S(1)}, s32[1,1,192]{2,1,0:T(1,128)}, u32[]{:S(2)}) copy-start(s32[1,1,192]{2,1,0:T(1,128)} %param.16) | copy-start | bytes 2308
  36.3 32.9 %copy-start.6 = (s32[1,1,192]{2,1,0:T(1,128)S(1)}, s32[1,1,192]{2,1,0:T(1,128)}, u32[]{:S(2)}) copy-start(s32[1,1,192]{2,1,0:T(1,128)} %param.15) | copy-start | bytes 2308
  69.2 80.4 %copy-start.8 = (bf16[256,256]{1,0:T(8,128)(2,1)S(1)}, bf16[256,256]{1,0:T(8,128)(2,1)}, u32[]{:S(2)}) copy-start(bf16[256,256]{1,0:T(8,128)(2,1)} %param.13) | copy-start | bytes 393220
  105.3 1.3 copy-start.4
  106.6 69.3 %all-gather.2.cloned.1.call-start = ((), (), s32[]{:S(2)}) async-start(), calls=%async_computation.5 | async-start | bytes 1179648 | tf_op jit(solution)/shard_map/all_gather | solution.py:63
  152.4 8.7 %copy-start.5 = (f32[256,256]{1,0:T(8,128)S(1)}, f32[256,256]{1,0:T(8,128)}, u32[]{:S(2)}) copy-start(f32[256,256]{1,0:T(8,128)} %reduce-scatter.3.cloned.1.call-done) | copy-start | bytes 786436
  152.4 105.0 %all-reduce.3.cloned.1.call-start = ((), (), s32[]{:S(2)}) async-start(), calls=%async_computation.3 | async-start | bytes 524288 | tf_op jit(solution)/shard_map/psum | solution.py:59
  162.0 122.7 %reduce-scatter.5.cloned.1.call-start = ((), (), s32[]{:S(2)}) async-start(), calls=%async_computation.6 | async-start | bytes 1310720 | tf_op jit(solution)/shard_map/reduce_scatter | solution.py:67
  176.0 11.6 %copy-start.3 = (bf16[2048,256]{1,0:T(8,128)(2,1)S(1)}, bf16[2048,256]{1,0:T(8,128)(2,1)}, u32[]{:S(2)}) copy-start(bf16[2048,256]{1,0:T(8,128)(2,1)} %all-gather.2.cloned.1.call-done) | copy-start | bytes 3145732
  220.3 102.5 %copy-start.1 = (bf16[256,256]{1,0:T(8,128)(2,1)S(1)}, bf16[256,256]{1,0:T(8,128)(2,1)}, u32[]{:S(2)}) copy-start(bf16[256,256]{1,0:T(8,128)(2,1)} %param.12) | copy-start | bytes 393220
  256.3 1.0 copy-start.2
  257.3 63.7 %all-reduce.5.cloned.1.call-start = ((), (), s32[]{:S(2)}) async-start(), calls=%async_computation.4 | async-start | bytes 524288 | tf_op jit(solution)/shard_map/psum | solution.py:59
Sparse Core Ops, SparseCore 0:
  106.7 42.8 reduce-scatter.2
  152.6 23.3 all-gather.1
  179.6 53.8 all-reduce.2
  257.5 27.2 reduce-scatter.4
  287.0 34.0 all-reduce.4
